TPU v7x, 32 devices: a whole 2x2x4 slice. The times are simulated.
32 devices in a mesh: dp: 8 (over y, x, core), tensor: 4 (over z).
Axes of the slice: x: 2, y: 2, z: 4, core: 2. Of those that a mesh axis runs over, the one named last changes fastest.
Arguments:
- inputs: bfloat16 [32768, 768], P('dp'), may hold values from -6 to 6
- segments: int32 [64, 512], P('dp'), may hold values from 0 to 7, never falling along the last dimension, each value on 1 to 128 neighbouring positions
- w_query: bfloat16 [768, 768], P(None, 'tensor'), may hold values from -0.21875 to 0.21875
- w_key: bfloat16 [768, 768], P(None, 'tensor'), may hold values from -0.21875 to 0.21875
- w_value: bfloat16 [768, 768], P(None, 'tensor'), may hold values from -0.21875 to 0.21875
- b_query: bfloat16 [768], P('tensor'), may hold values from -3 to 3
- b_value: bfloat16 [768], P('tensor'), may hold values from -3 to 3
- w_output: bfloat16 [768, 768], P('tensor'), may hold values from -0.875 to 0.875
- b_output: bfloat16 [768], replicated, may hold values from -3 to 3
- gain_attn: bfloat16 [768], replicated, may hold values from 0.5 to 1.5
- shift_attn: bfloat16 [768], replicated, may hold values from -3 to 3
- w_hidden: bfloat16 [768, 3072], P(None, 'tensor'), may hold values from -0.21875 to 0.21875
- b_hidden: bfloat16 [3072], P('tensor'), may hold values from -3 to 3
- w_project: bfloat16 [3072, 768], P('tensor'), may hold values from -0.109375 to 0.109375
- b_project: bfloat16 [768], replicated, may hold values from -3 to 3
- gain_ffn: bfloat16 [768], replicated, may hold values from 0.5 to 1.5
- shift_ffn: bfloat16 [768], replicated, may hold values from -3 to 3
- cotangent: bfloat16 [32768, 768], P(('dp', 'tensor')), may hold values from -6 to 6
Outputs:
- output: bfloat16 [32768, 768], P(('dp', 'tensor'))
- grad_input: float32 [32768, 768], P(('dp', 'tensor'))
- grad_w_query: float32 [768, 768], P('dp', 'tensor')
- grad_w_key: float32 [768, 768], P('dp', 'tensor')
- grad_w_value: float32 [768, 768], P('dp', 'tensor')
- grad_w_output: float32 [768, 768], P('tensor', 'dp')
- grad_w_hidden: float32 [768, 3072], P('dp', 'tensor')
- grad_w_project: float32 [3072, 768], P('tensor', 'dp')
- grad_bias_qv: float32 [2, 12, 64], P(None, 'tensor', 'dp')
- grad_b_hidden: float32 [48, 64], P('tensor', 'dp')
- grad_vectors: float32 [6, 768], P(None, ('dp', 'tensor'))
Inputs may be any that keep to these rules, and one draw needn't show every extreme that they name: `segments`: within each row of 512 tokens segment numbers never fall; each text holds 1 to 128 tokens, and some text holds exactly 128.
All inputs are finite; a program needn't handle non-finite values.
Results may differ from a plain program's by a relative error of at most 0.014.
Values may be sent and summed in bfloat16 or wider, within the bound.
A program may use at most 192 MiB of HBM per device.

v0:
```python
import jax
import jax.numpy as jnp
from jax import lax
from jax.sharding import PartitionSpec as P

HD = 64
norm_epsilon = 1e-12
root_half = 0.7071067811865476


def norm_forward(values, norm_gain, norm_shift):
    average = jnp.mean(values, axis=-1, keepdims=True)
    centered = values - average
    variance = jnp.mean(centered * centered, axis=-1, keepdims=True)
    inverse = lax.rsqrt(variance + norm_epsilon)
    scaled = centered * inverse
    return (scaled * norm_gain + norm_shift, scaled, inverse)


def norm_backward(grad_out, scaled, inverse, norm_gain):
    weighted = grad_out * norm_gain
    mean_grad = jnp.mean(weighted, axis=-1, keepdims=True)
    mean_proj = jnp.mean(weighted * scaled, axis=-1, keepdims=True)
    return inverse * (weighted - mean_grad - scaled * mean_proj)


def gelu_exact(values):
    return 0.5 * values * (1.0 + lax.erf(values * root_half))


def cross_rows(left, right):
    return lax.dot_general(
        left, right, (((0,), (0,)), ((), ())), preferred_element_type=jnp.float32
    )


def times_transposed(left, right):
    return lax.dot_general(
        left, right, (((1,), (1,)), ((), ())), preferred_element_type=jnp.float32
    )


def masked_scores(queries, keys_in, segment_row):
    same_text = segment_row[:, None] == segment_row[None, :]
    scores = jnp.einsum("qhd,khd->hqk", queries, keys_in, preferred_element_type=jnp.float32)
    scores = scores * queries.shape[2] ** (-0.5)
    return jnp.where(same_text[None], scores, -1000000000.0)


def attend_forward(packed):
    queries, keys_in, values, segment_row = packed
    scores = masked_scores(queries, keys_in, segment_row)
    row_max = jnp.max(scores, axis=-1, keepdims=True)
    exponent = jnp.exp(scores - row_max)
    row_total = jnp.sum(exponent, axis=-1, keepdims=True)
    attn_probs = (exponent / row_total).astype(jnp.bfloat16)
    mixed_heads = jnp.einsum("hqk,khd->qhd", attn_probs, values, preferred_element_type=jnp.float32)
    return (mixed_heads.astype(jnp.bfloat16), row_max + jnp.log(row_total))


def attend_backward(packed):
    queries, keys_in, values, segment_row, logsum, grad_mixed = packed
    score_scale = queries.shape[2] ** (-0.5)
    scores = masked_scores(queries, keys_in, segment_row)
    attn_probs = jnp.exp(scores - logsum)
    grad_probs = jnp.einsum("qhd,khd->hqk", grad_mixed, values, preferred_element_type=jnp.float32)
    grad_values = jnp.einsum(
        "hqk,qhd->khd",
        attn_probs.astype(jnp.bfloat16),
        grad_mixed,
        preferred_element_type=jnp.float32,
    )
    inner_sum = jnp.sum(attn_probs * grad_probs, axis=-1, keepdims=True)
    grad_scores = (attn_probs * (grad_probs - inner_sum)).astype(jnp.bfloat16)
    grad_queries = (
        jnp.einsum("hqk,khd->qhd", grad_scores, keys_in, preferred_element_type=jnp.float32)
        * score_scale
    )
    grad_keys = (
        jnp.einsum("hqk,qhd->khd", grad_scores, queries, preferred_element_type=jnp.float32)
        * score_scale
    )
    return (
        grad_queries.astype(jnp.bfloat16),
        grad_keys.astype(jnp.bfloat16),
        grad_values.astype(jnp.bfloat16),
    )


def per_device(
    inputs,
    segments,
    w_query,
    w_key,
    w_value,
    b_query,
    b_value,
    w_output,
    b_output,
    gain_attn,
    shift_attn,
    w_hidden,
    b_hidden,
    w_project,
    b_project,
    gain_ffn,
    shift_ffn,
    cotangent,
):
    seq_len = segments.shape[1]
    share_tokens = cotangent.shape[0]
    share_rows = share_tokens // seq_len
    width = inputs.shape[1]
    groups, parts = (lax.axis_size("tensor"), lax.axis_size("dp"))
    place, part = (lax.axis_index("tensor"), lax.axis_index("dp"))
    everyone = ("tensor", "dp")
    low = jnp.bfloat16
    wide = jnp.float32

    def gathered(shard):
        rows = shard.shape[0] // parts
        piece = lax.dynamic_slice_in_dim(shard, part * rows, rows, 0)
        return lax.all_gather(piece, everyone, axis=0, tiled=True)

    def bias_of(shard):
        return lax.all_gather(shard, "tensor", axis=0, tiled=True).astype(wide)

    tokens = lax.dynamic_slice_in_dim(inputs, place * share_tokens, share_tokens, 0)
    rows_segments = lax.dynamic_slice_in_dim(segments, place * share_rows, share_rows, 0)
    split = w_query.shape[1]
    w_in = gathered(jnp.concatenate([w_query, w_key, w_value], axis=1))
    w_in = (
        w_in.reshape(groups, width, 3, split)
        .transpose(1, 2, 0, 3)
        .reshape(width, 3 * groups * split)
    )
    w_out = gathered(w_output)
    w_up = gathered(w_hidden).reshape(groups, width, -1).transpose(1, 0, 2).reshape(width, -1)
    w_down = gathered(w_project)
    small = bias_of(jnp.concatenate([b_query, b_value, b_hidden])).reshape(groups, -1)
    bias_query = small[:, :split].reshape(-1)
    bias_value = small[:, split : 2 * split].reshape(-1)
    bias_hidden = small[:, 2 * split :].reshape(-1)
    full = groups * split
    head_shape = (share_rows, seq_len, full // HD, HD)
    attn_gain = gain_attn.astype(wide)
    attn_shift = shift_attn.astype(wide)
    attn_bias = b_output.astype(wide)
    ffn_gain = gain_ffn.astype(wide)
    ffn_shift = shift_ffn.astype(wide)
    ffn_bias = b_project.astype(wide)
    grad_out = cotangent.astype(wide)
    projected = jnp.dot(tokens, w_in, preferred_element_type=wide)
    queries = (projected[:, :full] + bias_query).astype(low)
    keys_in = projected[:, full : 2 * full].astype(low)
    values = (projected[:, 2 * full :] + bias_value).astype(low)
    query_heads = queries.reshape(head_shape)
    key_heads = keys_in.reshape(head_shape)
    value_heads = values.reshape(head_shape)
    mixed_heads, logsum = lax.map(
        attend_forward, (query_heads, key_heads, value_heads, rows_segments)
    )
    mixed = mixed_heads.reshape(share_tokens, full)
    hidden = tokens.astype(wide) + (jnp.dot(mixed, w_out, preferred_element_type=wide) + attn_bias)
    normed, scaled, inverse = norm_forward(hidden, attn_gain, attn_shift)
    normed_low = normed.astype(low)
    hidden_pre = jnp.dot(normed_low, w_up, preferred_element_type=wide) + bias_hidden
    active, gelu_pull = jax.vjp(gelu_exact, hidden_pre)
    active_low = active.astype(low)
    block_sum = normed + (jnp.dot(active_low, w_down, preferred_element_type=wide) + ffn_bias)
    output, scaled_out, inverse_out = norm_forward(block_sum, ffn_gain, ffn_shift)
    grad_sum = norm_backward(grad_out, scaled_out, inverse_out, ffn_gain)
    grad_ffn_gain = jnp.sum(grad_out * scaled_out, axis=0)
    grad_ffn_shift = jnp.sum(grad_out, axis=0)
    grad_sum_low = grad_sum.astype(low)
    grad_ffn_bias = jnp.sum(grad_sum_low.astype(wide), axis=0)
    grad_active = times_transposed(grad_sum_low, w_down)
    grad_w_down = cross_rows(grad_sum_low, active_low)
    grad_hidden_pre = gelu_pull(grad_active)[0].astype(low)
    grad_b_hidden = jnp.sum(grad_hidden_pre.astype(wide), axis=0)
    grad_w_up = cross_rows(normed_low, grad_hidden_pre)
    grad_normed = grad_sum + times_transposed(grad_hidden_pre, w_up)
    grad_hidden = norm_backward(grad_normed, scaled, inverse, attn_gain)
    grad_hidden_low = grad_hidden.astype(low)
    grad_attn_gain = jnp.sum(grad_normed * scaled, axis=0)
    grad_attn_shift = jnp.sum(grad_normed, axis=0)
    grad_attn_bias = jnp.sum(grad_hidden_low.astype(wide), axis=0)
    grad_w_out = cross_rows(grad_hidden_low, mixed)
    grad_mixed = times_transposed(grad_hidden_low, w_out).astype(low).reshape(head_shape)
    grad_q, grad_k, grad_v = lax.map(
        attend_backward, (query_heads, key_heads, value_heads, rows_segments, logsum, grad_mixed)
    )
    grad_q = grad_q.reshape(share_tokens, full)
    grad_k = grad_k.reshape(share_tokens, full)
    grad_v = grad_v.reshape(share_tokens, full)
    grad_projected = jnp.concatenate([grad_q, grad_k, grad_v], axis=1)
    grad_w_in = cross_rows(tokens, grad_projected)
    grad_b_query = jnp.sum(grad_q.astype(wide), axis=0)
    grad_b_value = jnp.sum(grad_v.astype(wide), axis=0)
    grad_input = grad_hidden + times_transposed(grad_projected, w_in)

    def scattered(grad):
        rows = grad.shape[0]
        grad = grad.reshape(rows, groups, -1).transpose(1, 0, 2).reshape(groups * rows, -1)
        return lax.psum_scatter(grad, everyone, scatter_dimension=0, tiled=True)

    sum_down = scattered(grad_w_down).T
    sum_up = scattered(grad_w_up)
    sum_out = scattered(grad_w_out).T
    sum_in = scattered(
        grad_w_in.reshape(width, 3, groups, split).transpose(0, 2, 1, 3).reshape(width, -1)
    )
    vectors = jnp.concatenate(
        [
            jnp.stack([grad_b_query, grad_b_value]).reshape(2 * groups, split),
            grad_b_hidden.reshape(-1, split),
            jnp.stack(
                [
                    grad_attn_gain,
                    grad_attn_shift,
                    grad_attn_bias,
                    grad_ffn_gain,
                    grad_ffn_shift,
                    grad_ffn_bias,
                ]
            ).reshape(-1, split),
        ],
        axis=0,
    )
    vectors = lax.psum(vectors, ("dp", "tensor"))
    bias_qv = vectors[: 2 * groups].reshape(2, groups, split // HD, HD)
    rest = vectors[2 * groups :]
    hid = bias_hidden.shape[0] // split
    bias_h = rest[:hid].reshape(groups, -1, HD)
    vec = rest[hid:].reshape(6, -1)
    piece = HD // parts
    bias_qv = lax.dynamic_slice_in_dim(bias_qv, place, 1, 1)[:, 0]
    bias_qv = lax.dynamic_slice_in_dim(bias_qv, part * piece, piece, 2)
    bias_h = lax.dynamic_slice_in_dim(bias_h, place, 1, 0)[0]
    bias_h = lax.dynamic_slice_in_dim(bias_h, part * piece, piece, 1)
    piece = width // (parts * groups)
    vec = lax.dynamic_slice_in_dim(vec, (part * groups + place) * piece, piece, 1)
    return (
        output.astype(low),
        grad_input,
        sum_in[:, :split],
        sum_in[:, split : 2 * split],
        sum_in[:, 2 * split :],
        sum_out,
        sum_up,
        sum_down,
        bias_qv,
        bias_h,
        vec,
    )


def solution(mesh):
    in_specs = (
        P("dp", None),
        P("dp", None),
        P(None, "tensor"),
        P(None, "tensor"),
        P(None, "tensor"),
        P("tensor"),
        P("tensor"),
        P("tensor", None),
        P(),
        P(),
        P(),
        P(None, "tensor"),
        P("tensor"),
        P("tensor", None),
        P(),
        P(),
        P(),
        P(("dp", "tensor"), None),
    )
    out_specs = (
        P(("dp", "tensor"), None),
        P(("dp", "tensor"), None),
        P("dp", "tensor"),
        P("dp", "tensor"),
        P("dp", "tensor"),
        P("tensor", "dp"),
        P("dp", "tensor"),
        P("tensor", "dp"),
        P(None, "tensor", "dp"),
        P("tensor", "dp"),
        P(None, ("dp", "tensor")),
    )
    return jax.shard_map(
        per_device, mesh=mesh, in_specs=in_specs, out_specs=out_specs, check_vma=False
    )
```

profile of v0, /device:TPU:0, one launch (start us, length us, event | category | flops | bytes accessed | tf_op | source)
XLA Modules:
  0.0 852.2 jit_solution(8184249609554273054)
XLA Ops:
  18.6 14.9 %all-gather = bf16[4,1,1152]{2,1,0:T(2,128)(2,1)S(1)} all-gather(bf16[1,1,1152]{2,1,0:T(2,128)(2,1)S(1)} %reshape.275), channel_id=1, replica_groups=mesh['dp'=8,'tensor'=4] {'tensor'}, dimensions={0}, use_global_device_ids=true | all-gather | bytes 11520 | tf_op jit(solution)/shard_map/all_gather | solution.py:126
  45.4 31.5 %all-gather.6.cloned.1.call-done = bf16[3072,576]{1,0:T(8,128)(2,1)} async-done(((bf16[96,576]{1,0:T(8,128)(2,1)}), bf16[3072,576]{1,0:T(8,128)(2,1)}) %all-gather.6.cloned.1.call-update) | async-done | bytes 3538960 | tf_op jit(solution)/shard_map/all_gather | solution.py:123
  76.9 6.0 copy.132
  82.9 7.7 reshape.246
  90.6 2.5 copy.133
  93.2 3.9 fusion.82
  102.4 2.4 reshape.251
  106.5 2.6 copy.136
  109.1 3.9 reshape.252
  113.0 2.9 copy.139
  115.8 2.6 copy.134
  118.4 3.9 reshape.250
  122.3 2.9 copy.137
  126.5 23.2 %while.26 = (s32[]{:T(128)}, bf16[2,512,12,64]{1,3,2,0:T(8,128)(2,1)}, f32[2,12,512,1]{2,1,3,0:T(8,128)S(1)}, bf16[2,512,12,64]{1,3,2,0:T(8,128)(2,1)}, s32[2,51...) while((s32[]{:T(128)}, ...), condition=%wide.region_3.4_spmd, body=%wide.region_0.3_spmd.sunk | while | flops 843704320 | bytes 42172516 | solution.py:160
  126.9 3.2 fusion.124
  130.1 2.6 fusion.125
  132.7 5.5 fusion.126
  138.4 3.2 fusion.124
  141.6 2.6 fusion.125
  144.2 5.5 fusion.126
  149.7 3.0 copy.140
  154.3 3.9 fusion.80
  160.3 38.9 %all-gather.10.cloned.1.call-done = bf16[3072,768]{1,0:T(8,128)(2,1)} async-done(((bf16[96,768]{1,0:T(8,128)(2,1)}), bf16[3072,768]{1,0:T(8,128)(2,1)}) %all-gather.10.cloned.1.call-update) | async-done | bytes 4718608 | tf_op jit(solution)/shard_map/all_gather | solution.py:123
  199.2 6.8 copy.141
  206.0 13.7 %multiply_convert_fusion.3 = (bf16[1024,3072]{1,0:T(8,128)(2,1)}, f32[1024,3072]{1,0:T(8,128)}) fusion(f32[3072]{0:T(1024)S(1)} %copy-done.34, bf16[768,3072]{0,1:T(8,128)(2,1)} %bitcast.212, f32[1024,768]{0,1:T(8,128)} %copy-done.9, f32[768]{0:T(1024)S(1)} %copy-done.37, f32[768]{0:T(1024)S(1)} %copy-done.26, f32[1024]{0:T(1024)S(1)} %add_rsqrt_fusion.1, ...), kind=kOutput, calls=%fused_computation.66 | convolution fusion | flops 4854644736 | bytes 26765312 | tf_op jit(solution)/shard_map/dot_general | solution.py:167
  219.7 44.8 %all-gather.12.cloned.1.call-done = bf16[3072,768]{1,0:T(8,128)(2,1)} async-done(((bf16[96,768]{1,0:T(8,128)(2,1)}), bf16[3072,768]{1,0:T(8,128)(2,1)}) %all-gather.12.cloned.1.call-update) | async-done | bytes 4718608 | tf_op jit(solution)/shard_map/all_gather | solution.py:123
  264.5 9.4 %fusion.81 = (f32[1024]{0:T(1024)S(1)}, f32[1024,768]{0,1:T(8,128)S(1)}) fusion(f32[768]{0:T(1024)S(1)} %copy-done.39, bf16[1024,3072]{1,0:T(8,128)(2,1)} %get-tuple-element.280, bf16[3072,768]{1,0:T(8,128)(2,1)} %all-gather.12.cloned.1.call-done, f32[768]{0:T(1024)S(1)} %copy-done.37, f32[768]{0:T(1024)S(1)} %copy-done.26, f32[1024]{0:T(1024)S(1)} %add_rsqrt_fusion.1, ...), kind=kOutput, calls=%fused_computation.141 | convolution fusion | flops 4837342208 | bytes 17323008 | tf_op jit(solution)/shard_map/dot_general | solution.py:170
  277.3 3.3 convert_reduce_fusion.2
  280.6 15.2 %convert_reduce_fusion = (f32[3072]{0:T(1024)}, bf16[1024,3072]{1,0:T(8,128)(2,1)}) fusion(bf16[1024,768]{0,1:T(8,128)(2,1)S(1)} %get-tuple-element.263, bf16[3072,768]{1,0:T(8,128)(2,1)S(1)} %copy-done.45, f32[1024,3072]{1,0:T(8,128)} %get-tuple-element.281, f32[3072]{0:T(1024)S(1)} %copy-done.34), kind=kOutput, calls=%fused_computation.64 | convolution fusion | flops 4882166784 | bytes 25190400 | tf_op jit(solution)/shard_map/dot_general | solution.py:38
  295.9 11.2 %multiply_reduce_fusion.1 = (f32[768]{0:T(1024)}, f32[1024]{0:T(1024)S(1)}, f32[1024]{0:T(1024)S(1)}, f32[768]{0:T(1024)}, f32[1024,768]{0,1:T(8,128)}) fusion(f32[1024,768]{0,1:T(8,128)S(1)} %copy-done.10, f32[1024]{0:T(1024)S(1)} %add_rsqrt_fusion.1, f32[1024]{0:T(1024)S(1)} %broadcast_multiply_fusion.5, f32[768]{0:T(1024)S(1)} %copy-done.26, ...), kind=kOutput, calls=%fused_computation.85 | convolution fusion | flops 4845989888 | bytes 22065152 | tf_op jit(solution)/shard_map/dot_general | solution.py:38
  307.1 3.7 convert_reduce_fusion.3
  312.6 2.6 convolution_convert_fusion
  315.2 2.6 copy.145
  317.8 3.8 reshape.256
  321.6 3.1 copy.148
  324.7 4.3 convolution_bitcast_fusion
  329.0 3.4 copy.183
  336.5 52.0 %while.27 = (s32[]{:T(128)}, bf16[2,512,12,64]{1,3,2,0:T(8,128)(2,1)}, bf16[2,512,12,64]{1,3,2,0:T(8,128)(2,1)}, bf16[2,512,12,64]{1,3,2,0:T(8,128)(2,1)}, bf16[...) while((s32[]{:T(128)}, ...), condition=%wide.region_14.15_spmd, body=%wide.region_12.14_spmd.sunk | while | flops 2062673920 | bytes 147524944 | solution.py:190
  336.9 3.1 fusion.135
  340.0 3.9 fusion.138
  344.0 6.8 multiply_reduce_fusion.7
  350.8 7.3 multiply_convert_fusion.5
  362.7 3.1 fusion.135
  365.8 4.0 fusion.138
  369.8 6.9 multiply_reduce_fusion.7
  376.7 7.2 multiply_convert_fusion.5
  388.4 3.1 copy.151
  391.9 3.2 copy.152
  399.1 3.9 fusion.84
  403.0 3.3 copy.155
  406.4 8.4 copy.182
  415.5 10.8 %fusion.73 = f32[768,3072]{1,0:T(8,128)} fusion(bf16[1024,3072]{1,0:T(8,128)(2,1)} %get-tuple-element.286, f32[1024,768]{0,1:T(8,128)} %copy-done.9, f32[768]{0:T(1024)S(1)} %copy-done.38, f32[768]{0:T(1024)S(1)} %copy-done.27, f32[1024]{0:T(1024)S(1)} %copy-done.29, f32[1024]{0:T(1024)S(1)} %copy-done.22), kind=kOutput, calls=%fused_computation.136 | convolution fusion | flops 4835770368 | bytes 18888704 | tf_op jit(solution)/shard_map/dot_general | solution.py:32
  426.3 12.5 %reshape.263 = f32[768,4,768]{2,1,0:T(4,128)} reshape(f32[768,3072]{1,0:T(8,128)} %fusion.73) | data formatting | bytes 18874368 | tf_op jit(solution)/shard_map/reshape | solution.py:204
  438.8 9.2 %copy.159 = f32[4,768,768]{2,1,0:T(8,128)} copy(f32[4,768,768]{2,0,1:T(4,128)} %bitcast.197) | data formatting | bytes 18874368 | tf_op jit(solution)/shard_map/transpose | solution.py:204
  448.0 10.0 %fusion.83 = f32[768,3072]{1,0:T(8,128)} fusion(bf16[1024,768]{0,1:T(8,128)(2,1)} %copy-done.19, bf16[1024,3072]{1,0:T(8,128)(2,1)} %get-tuple-element.280), kind=kOutput, calls=%fused_computation.143 | convolution fusion | flops 4831838208 | bytes 17301504 | tf_op jit(solution)/shard_map/dot_general | solution.py:32
  458.0 12.7 %reshape.265 = f32[768,4,768]{2,1,0:T(4,128)} reshape(f32[768,3072]{1,0:T(8,128)} %fusion.83) | data formatting | bytes 18874368 | tf_op jit(solution)/shard_map/reshape | solution.py:204
  470.8 9.5 %copy.160 = f32[4,768,768]{2,1,0:T(8,128)} copy(f32[4,768,768]{2,0,1:T(4,128)} %bitcast.198) | data formatting | bytes 18874368 | tf_op jit(solution)/shard_map/transpose | solution.py:204
  483.5 41.2 %psum.7 = f32[48,192]{1,0:T(8,128)S(1)} all-reduce(f32[48,192]{1,0:T(8,128)S(1)} %pad_maximum_fusion), channel_id=1, replica_groups=mesh['dp'=8,'tensor'=4] {'dp','tensor'}, use_global_device_ids=true, to_apply=%region_28.29 | all-reduce | flops 9216 | bytes 73728 | tf_op jit(solution)/shard_map/psum | solution.py:230
  526.3 2.6 copy.163
  528.9 10.0 %convolution_add_fusion.1 = f32[1024,768]{0,1:T(8,128)} fusion(f32[1024,768]{0,1:T(8,128)} %copy-done.16, bf16[1024,2304]{0,1:T(8,128)(2,1)} %copy-done.20, bf16[768,2304]{0,1:T(8,128)(2,1)} %bitcast.217), kind=kOutput, calls=%fused_computation.101 | convolution fusion | flops 3624665088 | bytes 14548992 | tf_op jit(solution)/shard_map/dot_general | solution.py:38
  538.9 3.5 copy.164
  544.8 16.7 %reduce-scatter.13.cloned.1.call-done = f32[96,576]{1,0:T(8,128)} async-done(((f32[3072,576]{1,0:T(8,128)}), f32[96,576]{1,0:T(8,128)}) %reduce-scatter.13.cloned.1.call-update) | async-done | bytes 221200
  563.2 139.7 %reduce-scatter.9.cloned.1.call-done = f32[96,768]{1,0:T(8,128)} async-done(((f32[3072,768]{1,0:T(8,128)}), f32[96,768]{1,0:T(8,128)}) %reduce-scatter.9.cloned.1.call-update) | async-done | bytes 294928 | tf_op jit(solution)/shard_map/reduce_scatter | solution.py:205
  703.0 141.8 %reduce-scatter.11.cloned.1.call-done = f32[96,768]{1,0:T(8,128)} async-done(((f32[3072,768]{1,0:T(8,128)}), f32[96,768]{1,0:T(8,128)}) %reduce-scatter.11.cloned.1.call-update) | async-done | bytes 294928 | tf_op jit(solution)/shard_map/reduce_scatter | solution.py:205
  (228 shorter events, 67.8 us)
Async XLA Ops:
  7.2 7.5 copy-start
  7.2 9.9 %copy-start.41 = (bf16[768]{0:T(1024)(128)(2,1)S(1)}, bf16[768]{0:T(1024)(128)(2,1)}, u32[]{:S(2)}) copy-start(bf16[768]{0:T(1024)(128)(2,1)} %param.34) | copy-start | bytes 4612
  7.2 26.3 %copy-start.42 = (bf16[768]{0:T(1024)(128)(2,1)S(1)}, bf16[768]{0:T(1024)(128)(2,1)}, u32[]{:S(2)}) copy-start(bf16[768]{0:T(1024)(128)(2,1)} %param.31) | copy-start | bytes 4612
  7.2 26.9 %copy-start.43 = (bf16[768]{0:T(1024)(128)(2,1)S(1)}, bf16[768]{0:T(1024)(128)(2,1)}, u32[]{:S(2)}) copy-start(bf16[768]{0:T(1024)(128)(2,1)} %param.32) | copy-start | bytes 4612
  7.2 27.5 %copy-start.44 = (bf16[768]{0:T(1024)(128)(2,1)S(1)}, bf16[768]{0:T(1024)(128)(2,1)}, u32[]{:S(2)}) copy-start(bf16[768]{0:T(1024)(128)(2,1)} %param.37) | copy-start | bytes 4612
  7.2 32.7 %copy-start.18 = (bf16[1024,768]{1,0:T(8,128)(2,1)S(1)}, bf16[1024,768]{1,0:T(8,128)(2,1)}, u32[]{:S(2)}) copy-start(bf16[1024,768]{1,0:T(8,128)(2,1)} %param.39) | copy-start | bytes 4718596
  7.2 69.7 %all-gather.6.cloned.1.call-start = ((), (), s32[]{:S(2)}) async-start(), calls=%async_computation.4 | async-start | bytes 4055040 | tf_op jit(solution)/shard_map/all_gather | solution.py:123
  13.2 141.2 %all-gather.8.cloned.1.call-start = ((), (), s32[]{:S(2)}) async-start(), calls=%async_computation.5 | async-start | bytes 1216512 | tf_op jit(solution)/shard_map/all_gather | solution.py:123
  14.6 184.6 %all-gather.10.cloned.1.call-start = ((), (), s32[]{:S(2)}) async-start(), calls=%async_computation.6 | async-start | bytes 4866048 | tf_op jit(solution)/shard_map/all_gather | solution.py:123
  15.4 249.1 %all-gather.12.cloned.1.call-start = ((), (), s32[]{:S(2)}) async-start(), calls=%async_computation.7 | async-start | bytes 4866048 | tf_op jit(solution)/shard_map/all_gather | solution.py:123
  17.1 526.1 %reduce-scatter.15.cloned.1.call-start = ((), (), s32[]{:S(2)}) async-start(), calls=%async_computation.11 | async-start | bytes 3244032
  43.1 50.1 %copy-start.13 = (bf16[1024,768]{1,0:T(8,128)(2,1)}, bf16[1024,768]{1,0:T(8,128)(2,1)S(1)}, u32[]{:S(2)}) copy-start(bf16[1024,768]{1,0:T(8,128)(2,1)S(1)} %constant_dynamic-slice_fusion.9) | copy-start | bytes 4718596
  93.2 3.9 copy-start.15
  149.7 4.6 copy-start.40
  158.2 1.7 copy-start.9
  158.3 148.9 %copy-start.21 = (f32[1024]{0:T(1024)}, f32[1024]{0:T(1024)S(1)}, u32[]{:S(2)}) copy-start(f32[1024]{0:T(1024)S(1)} %broadcast_multiply_fusion.5) | copy-start | bytes 12292
  160.3 146.8 %copy-start.28 = (f32[1024]{0:T(1024)}, f32[1024]{0:T(1024)S(1)}, u32[]{:S(2)}) copy-start(f32[1024]{0:T(1024)S(1)} %add_rsqrt_fusion.1) | copy-start | bytes 12292
  199.2 6.8 copy-start.26
  199.2 6.8 copy-start.34
  199.2 6.8 copy-start.37
  206.0 58.5 %copy-start.39 = (f32[768]{0:T(1024)S(1)}, f32[768]{0:T(1024)}, u32[]{:S(2)}) copy-start(f32[768]{0:T(1024)} %convert_element_type.111) | copy-start | bytes 9220
  273.9 1.4 copy-start.8
  274.0 1.4 copy-start.23
  274.4 3.0 copy-start.30
  275.4 5.2 copy-start.45
  277.3 18.5 %slice-start = ((s8[4718592]{0:T(1024)(128)(4,1)}), s8[4194304]{0:T(1024)(128)(4,1)S(1)}, s32[]{:S(2)}) async-start(s8[4718592]{0:T(1024)(128)(4,1)} %bitcast.213), calls=%async_computation.12 | async-start | bytes 8388608
  280.6 15.3 %copy-start.19 = (bf16[1024,768]{0,1:T(8,128)(2,1)}, bf16[1024,768]{0,1:T(8,128)(2,1)S(1)}, u32[]{:S(2)}) copy-start(bf16[1024,768]{0,1:T(8,128)(2,1)S(1)} %get-tuple-element.263) | copy-start | bytes 4718596
  280.6 15.3 %copy-start.10 = (f32[1024,768]{0,1:T(8,128)S(1)}, f32[1024,768]{0,1:T(8,128)}, u32[]{:S(2)}) copy-start(f32[1024,768]{0,1:T(8,128)} %copy-done.9) | copy-start | bytes 9437188
  280.6 15.3 %slice-start.1 = ((s8[4718592]{0:T(1024)(128)(4,1)}), s8[524288]{0:T(1024)(128)(4,1)S(1)}, s32[]{:S(2)}) async-start(s8[4718592]{0:T(1024)(128)(4,1)} %bitcast.213), calls=%async_computation.13 | async-start | bytes 1048576
  307.1 5.5 copy-start.46
  310.9 1.7 copy-start.16
  321.6 3.1 copy-start.17
  332.5 229.0 %reduce-scatter.13.cloned.1.call-start = ((), (), s32[]{:S(2)}) async-start(), calls=%async_computation.10 | async-start | bytes 8110080
  336.9 3.1 copy-start.4
  340.0 4.0 copy-start.3
  350.8 7.3 copy-start.11
  358.1 2.0 copy-start.2
  358.1 2.0 copy-start.5
  360.2 1.1 copy-start.12
  361.3 1.1 copy-start.6
  362.7 3.1 copy-start.4
  365.8 4.0 copy-start.3
  376.7 7.2 copy-start.11
  383.9 2.0 copy-start.2
  383.9 2.0 copy-start.5
  385.9 1.1 copy-start.12
  387.1 1.1 copy-start.6
  391.9 3.6 copy-start.7
  397.7 1.4 copy-start.14
  399.1 3.9 copy-start.20
  414.8 0.7 copy-start.22
  414.8 0.7 copy-start.27
  414.8 0.7 copy-start.29
  414.8 0.7 copy-start.38
  414.8 288.2 %reduce-scatter.9.cloned.1.call-start = ((), (), s32[]{:S(2)}) async-start(), calls=%async_computation.8 | async-start | bytes 9732096 | tf_op jit(solution)/shard_map/reduce_scatter | solution.py:205
  448.0 396.8 %reduce-scatter.11.cloned.1.call-start = ((), (), s32[]{:S(2)}) async-start(), calls=%async_computation.9 | async-start | bytes 9732096 | tf_op jit(solution)/shard_map/reduce_scatter | solution.py:205
  480.3 0.7 copy-start.32
  480.3 0.7 copy-start.31
  480.3 0.7 copy-start.36
  480.3 0.7 copy-start.24
  480.3 0.7 copy-start.35
  480.3 0.8 copy-start.25
  480.3 0.8 copy-start.33
  528.9 315.9 %copy-start.1 = (bf16[768,768]{1,0:T(8,128)(2,1)S(1)}, bf16[768,768]{1,0:T(8,128)(2,1)}, u32[]{:S(2)}) copy-start(bf16[768,768]{1,0:T(8,128)(2,1)} %param.33) | copy-start | bytes 3538948
Sparse Core Ops, SparseCore 0:
  13.3 63.5 all-gather.5
  80.4 52.7 all-gather.7
  136.7 62.4 all-gather.9
  202.5 61.9 all-gather.11
  332.6 100.4 reduce-scatter.14
  438.6 122.7 reduce-scatter.12
  567.9 135.0 reduce-scatter.8
  709.5 135.3 reduce-scatter.10
where the time goes:
time: 862 us; the launch traced here: 852 us
  waiting for transfers between devices  414 us (48%)
  local copies, waits for them, and re-layouts  174 us (20%)
  matrix products  150 us (17%)
  blocking collectives  56.1 us (7%)
  other arithmetic  41.7 us (5%)
  between operations  15.3 us (2%)
    reduce_scatter x2, waiting for transfers between devices, scattered(): return lax.psum_scatter(grad, everyone, scatter_dimension=0, tiled=True)  282 us
    all_gather x4, waiting for transfers between devices, gathered(): return lax.all_gather(piece, everyone, axis=0, tiled=True)  115 us
    psum x1, blocking collectives, per_device(): vectors = lax.psum(vectors, ('dp', 'tensor'))  41.2 us
    dot_general x4, matrix products, times_transposed(): lax.dot_general(left, right, (((1,), (1,)), ((), ())), preferred_element_...  39.1 us
    unnamed x103, local copies, waits for them, and re-layouts  38.6 us
    dot_general x4, matrix products, cross_rows(): lax.dot_general(left, right, (((0,), (0,)), ((), ())), preferred_element_...  29 us
    reshape x2, local copies, waits for them, and re-layouts, scattered(): grad.reshape(rows, groups, -1).transpose(1, 0, 2).reshape(groups * rows, -1)  25.2 us
    transpose x2, local copies, waits for them, and re-layouts, scattered(): grad.reshape(rows, groups, -1).transpose(1, 0, 2).reshape(groups * rows, -1)  18.7 us
  transfers between devices with their start and end apart: 8, of which 6 were waited for; matrix products, arithmetic and copies ran while one was open for 34% of the time, Pallas kernels for 0%

commit v1 on v0

--- a/solution.py
+++ b/solution.py
@@ -227,7 +227,7 @@
         ],
         axis=0,
     )
-    vectors = lax.psum(vectors, ("dp", "tensor"))
+    vectors = jnp.sum(lax.all_gather(vectors, ("dp", "tensor")), axis=0)
     bias_qv = vectors[: 2 * groups].reshape(2, groups, split // HD, HD)
     rest = vectors[2 * groups :]
     hid = bias_hidden.shape[0] // split

time: 862 us -> 973 us (1.13)
  waiting for transfers between devices: 414 us -> 565 us
  blocking collectives: 56.1 us -> 14.9 us
    unnamed x10 -> x11, waiting for transfers between devices: 16.8 us -> 168 us
    psum x1 -> x0, blocking collectives: 41.2 us -> none  [per_device(): vectors = lax.psum(vectors, ('dp', 'tensor'))]
    unnamed x103 -> x93, local copies, waits for them, and re-layouts: 38.6 us -> 36.6 us
  transfers between devices with their start and end apart: 8 -> 9, of which waited for: 6 -> 7; matrix products, arithmetic and copies ran while one was open for 34% -> 24% of each run, Pallas kernels for 0% -> 0%
where the time goes in v1:
time: 973 us; the launch traced here: 963 us
  waiting for transfers between devices  565 us (58%)
  local copies, waits for them, and re-layouts  171 us (18%)
  matrix products  151 us (16%)
  other arithmetic  44.7 us (5%)
  blocking collectives  14.9 us (2%)
  between operations  14.6 us (2%)
    reduce_scatter x2, waiting for transfers between devices, scattered(): return lax.psum_scatter(grad, everyone, scatter_dimension=0, tiled=True)  281 us
    unnamed x11, waiting for transfers between devices  168 us
    all_gather x4, waiting for transfers between devices, gathered(): return lax.all_gather(piece, everyone, axis=0, tiled=True)  115 us
    dot_general x4, matrix products, times_transposed(): lax.dot_general(left, right, (((1,), (1,)), ((), ())), preferred_element_...  40.2 us
    unnamed x93, local copies, waits for them, and re-layouts  36.6 us
    dot_general x4, matrix products, cross_rows(): lax.dot_general(left, right, (((0,), (0,)), ((), ())), preferred_element_...  28.4 us
    reshape x2, local copies, waits for them, and re-layouts, scattered(): grad.reshape(rows, groups, -1).transpose(1, 0, 2).reshape(groups * rows, -1)  25 us
  transfers between devices with their start and end apart: 9, of which 7 were waited for; matrix products, arithmetic and copies ran while one was open for 24% of the time, Pallas kernels for 0%

profile of v1, /device:TPU:0, one launch (start us, length us, event | category | flops | bytes accessed | tf_op | source)
XLA Modules:
  0.0 962.9 jit_solution(15766987510544026565)
XLA Ops:
  18.6 14.9 %all-gather.1 = bf16[4,1,1152]{2,1,0:T(2,128)(2,1)S(1)} all-gather(bf16[1,1,1152]{2,1,0:T(2,128)(2,1)S(1)} %reshape.276), channel_id=1, replica_groups=mesh['dp'=8,'tensor'=4] {'tensor'}, dimensions={0}, use_global_device_ids=true | all-gather | bytes 11520 | tf_op jit(solution)/shard_map/all_gather | solution.py:126
  45.4 31.5 %all-gather.8.cloned.1.call-done = bf16[3072,576]{1,0:T(8,128)(2,1)} async-done(((bf16[96,576]{1,0:T(8,128)(2,1)}), bf16[3072,576]{1,0:T(8,128)(2,1)}) %all-gather.8.cloned.1.call-update) | async-done | bytes 3538960 | tf_op jit(solution)/shard_map/all_gather | solution.py:123
  76.9 6.0 copy.176
  82.9 7.7 reshape.246
  90.6 2.5 copy.177
  93.1 3.9 fusion.82
  98.3 2.3 fusion.64
  102.4 2.4 reshape.251
  106.5 2.6 copy.180
  109.0 3.9 reshape.252
  112.9 2.9 copy.183
  115.8 2.6 copy.178
  118.4 3.9 reshape.250
  122.3 2.9 copy.181
  126.5 23.2 %while.26 = (s32[]{:T(128)}, bf16[2,512,12,64]{1,3,2,0:T(8,128)(2,1)}, f32[2,12,512,1]{2,1,3,0:T(8,128)S(1)}, bf16[2,512,12,64]{1,3,2,0:T(8,128)(2,1)}, s32[2,51...) while((s32[]{:T(128)}, ...), condition=%wide.region_3.4_spmd, body=%wide.region_0.3_spmd.sunk | while | flops 843704320 | bytes 42172516 | solution.py:160
  126.9 3.2 fusion.124
  130.1 2.6 fusion.125
  132.7 5.5 fusion.126
  138.4 3.2 fusion.124
  141.6 2.6 fusion.125
  144.2 5.5 fusion.126
  149.7 3.0 copy.184
  154.4 3.9 fusion.80
  160.3 38.9 %all-gather.12.cloned.1.call-done = bf16[3072,768]{1,0:T(8,128)(2,1)} async-done(((bf16[96,768]{1,0:T(8,128)(2,1)}), bf16[3072,768]{1,0:T(8,128)(2,1)}) %all-gather.12.cloned.1.call-update) | async-done | bytes 4718608 | tf_op jit(solution)/shard_map/all_gather | solution.py:123
  199.2 6.7 copy.185
  205.9 13.7 %multiply_convert_fusion.3 = (bf16[1024,3072]{1,0:T(8,128)(2,1)}, f32[1024,3072]{1,0:T(8,128)}) fusion(f32[3072]{0:T(1024)S(1)} %copy-done.32, bf16[768,3072]{0,1:T(8,128)(2,1)} %bitcast.213, f32[1024,768]{0,1:T(8,128)} %copy-done.9, f32[768]{0:T(1024)S(1)} %copy-done.33, f32[768]{0:T(1024)S(1)} %copy-done.27, f32[1024]{0:T(1024)S(1)} %add_rsqrt_fusion.1, ...), kind=kOutput, calls=%fused_computation.66 | convolution fusion | flops 4854644736 | bytes 26765312 | tf_op jit(solution)/shard_map/dot_general | solution.py:167
  219.6 44.8 %all-gather.14.cloned.1.call-done = bf16[3072,768]{1,0:T(8,128)(2,1)} async-done(((bf16[96,768]{1,0:T(8,128)(2,1)}), bf16[3072,768]{1,0:T(8,128)(2,1)}) %all-gather.14.cloned.1.call-update) | async-done | bytes 4718608 | tf_op jit(solution)/shard_map/all_gather | solution.py:123
  264.5 9.4 fusion.81
  276.7 2.6 convert_reduce_fusion.2
  279.4 14.7 %convert_reduce_fusion = (f32[3072]{0:T(1024)S(1)}, bf16[1024,3072]{1,0:T(8,128)(2,1)}) fusion(bf16[1024,768]{0,1:T(8,128)(2,1)S(1)} %get-tuple-element.291, bf16[3072,768]{1,0:T(8,128)(2,1)S(1)} %copy-done.41, f32[1024,3072]{1,0:T(8,128)} %get-tuple-element.309, f32[3072]{0:T(1024)S(1)} %copy-done.32), kind=kOutput, calls=%fused_computation.64 | convolution fusion | flops 4882166784 | bytes 25190400 | tf_op jit(solution)/shard_map/dot_general | solution.py:38
  294.1 10.6 %multiply_reduce_fusion.1 = (f32[768]{0:T(1024)S(1)}, f32[1024]{0:T(1024)S(1)}, f32[1024]{0:T(1024)S(1)}, f32[768]{0:T(1024)S(1)}, f32[1024,768]{0,1:T(8,128)}) fusion(f32[1024,768]{0,1:T(8,128)S(1)} %copy-done.10, f32[1024]{0:T(1024)S(1)} %add_rsqrt_fusion.1, f32[1024]{0:T(1024)S(1)} %broadcast_multiply_fusion.5, f32[768]{0:T(1024)S(1)} %copy-done.27, ...), kind=kOutput, calls=%fused_computation.85 | convolution fusion | flops 4845989888 | bytes 22065152 | tf_op jit(solution)/shard_map/dot_general | solution.py:38
  304.8 4.7 convert_reduce_fusion.3
  310.9 4.9 convolution_convert_fusion
  315.8 2.6 copy.189
  318.4 3.9 reshape.256
  322.2 2.9 copy.192
  329.2 51.7 %while.27 = (s32[]{:T(128)}, bf16[2,512,12,64]{1,3,2,0:T(8,128)(2,1)}, bf16[2,512,12,64]{1,3,2,0:T(8,128)(2,1)}, bf16[2,512,12,64]{1,3,2,0:T(8,128)(2,1)}, bf16[...) while((s32[]{:T(128)}, ...), condition=%wide.region_14.15_spmd, body=%wide.region_12.14_spmd.sunk | while | flops 2062673920 | bytes 147524944 | solution.py:190
  329.7 3.1 fusion.135
  332.8 4.0 fusion.138
  336.8 6.9 multiply_reduce_fusion.7
  343.6 7.1 multiply_convert_fusion.5
  355.4 3.1 fusion.135
  358.5 4.0 fusion.138
  362.5 6.9 multiply_reduce_fusion.7
  369.4 7.1 multiply_convert_fusion.5
  376.5 2.0 fusion.137
  385.3 3.8 convolution_bitcast_fusion
  389.1 2.3 copy.227
  391.9 3.2 copy.196
  401.1 3.9 fusion.84
  405.0 3.4 copy.199
  408.4 8.3 copy.226
  417.4 10.5 %fusion.73 = f32[768,3072]{1,0:T(8,128)} fusion(bf16[1024,3072]{1,0:T(8,128)(2,1)} %get-tuple-element.314, f32[1024,768]{0,1:T(8,128)} %copy-done.9, f32[768]{0:T(1024)S(1)} %copy-done.34, f32[768]{0:T(1024)S(1)} %copy-done.28, f32[1024]{0:T(1024)S(1)} %copy-done.30, f32[1024]{0:T(1024)S(1)} %copy-done.25), kind=kOutput, calls=%fused_computation.136 | convolution fusion | flops 4835770368 | bytes 18888704 | tf_op jit(solution)/shard_map/dot_general | solution.py:32
  427.9 12.4 %reshape.263 = f32[768,4,768]{2,1,0:T(4,128)} reshape(f32[768,3072]{1,0:T(8,128)} %fusion.73) | data formatting | bytes 18874368 | tf_op jit(solution)/shard_map/reshape | solution.py:204
  440.3 9.2 copy.203
  450.9 10.2 %fusion.83 = f32[768,3072]{1,0:T(8,128)} fusion(bf16[1024,768]{0,1:T(8,128)(2,1)S(1)} %copy-done.20, bf16[1024,3072]{1,0:T(8,128)(2,1)} %get-tuple-element.308), kind=kOutput, calls=%fused_computation.143 | convolution fusion | flops 4831838208 | bytes 17301504 | tf_op jit(solution)/shard_map/dot_general | solution.py:32
  461.2 12.6 %reshape.265 = f32[768,4,768]{2,1,0:T(4,128)} reshape(f32[768,3072]{1,0:T(8,128)} %fusion.83) | data formatting | bytes 18874368 | tf_op jit(solution)/shard_map/reshape | solution.py:204
  473.7 9.3 copy.204
  486.0 10.0 %convolution_add_fusion.1 = f32[1024,768]{0,1:T(8,128)} fusion(f32[1024,768]{0,1:T(8,128)} %get-tuple-element.293, bf16[1024,2304]{0,1:T(8,128)(2,1)} %copy-done.21, bf16[768,2304]{0,1:T(8,128)(2,1)} %bitcast.218), kind=kOutput, calls=%fused_computation.101 | convolution fusion | flops 3624665088 | bytes 14548992 | tf_op jit(solution)/shard_map/dot_general | solution.py:38
  496.0 3.5 copy.208
  503.4 41.7 %reduce-scatter.15.cloned.1.call-done = f32[96,192]{1,0:T(8,128)} async-done(((f32[3072,192]{1,0:T(8,128)}), f32[96,192]{1,0:T(8,128)}) %reduce-scatter.15.cloned.1.call-update) | async-done | bytes 73744
  546.7 126.2 %reduce-scatter.13.cloned.1.call-done = f32[96,576]{1,0:T(8,128)} async-done(((f32[3072,576]{1,0:T(8,128)}), f32[96,576]{1,0:T(8,128)}) %reduce-scatter.13.cloned.1.call-update) | async-done | bytes 221200
  674.8 139.8 %reduce-scatter.9.cloned.1.call-done = f32[96,768]{1,0:T(8,128)} async-done(((f32[3072,768]{1,0:T(8,128)}), f32[96,768]{1,0:T(8,128)}) %reduce-scatter.9.cloned.1.call-update) | async-done | bytes 294928 | tf_op jit(solution)/shard_map/reduce_scatter | solution.py:205
  814.5 141.6 %reduce-scatter.11.cloned.1.call-done = f32[96,768]{1,0:T(8,128)} async-done(((f32[3072,768]{1,0:T(8,128)}), f32[96,768]{1,0:T(8,128)}) %reduce-scatter.11.cloned.1.call-update) | async-done | bytes 294928 | tf_op jit(solution)/shard_map/reduce_scatter | solution.py:205
  (221 shorter events, 71.9 us)
Async XLA Ops:
  7.2 7.5 copy-start
  7.2 9.9 %copy-start.37 = (bf16[768]{0:T(1024)(128)(2,1)S(1)}, bf16[768]{0:T(1024)(128)(2,1)}, u32[]{:S(2)}) copy-start(bf16[768]{0:T(1024)(128)(2,1)} %param.34) | copy-start | bytes 4612
  7.2 26.3 %copy-start.38 = (bf16[768]{0:T(1024)(128)(2,1)S(1)}, bf16[768]{0:T(1024)(128)(2,1)}, u32[]{:S(2)}) copy-start(bf16[768]{0:T(1024)(128)(2,1)} %param.31) | copy-start | bytes 4612
  7.2 26.9 %copy-start.39 = (bf16[768]{0:T(1024)(128)(2,1)S(1)}, bf16[768]{0:T(1024)(128)(2,1)}, u32[]{:S(2)}) copy-start(bf16[768]{0:T(1024)(128)(2,1)} %param.32) | copy-start | bytes 4612
  7.2 27.5 %copy-start.40 = (bf16[768]{0:T(1024)(128)(2,1)S(1)}, bf16[768]{0:T(1024)(128)(2,1)}, u32[]{:S(2)}) copy-start(bf16[768]{0:T(1024)(128)(2,1)} %param.37) | copy-start | bytes 4612
  7.2 32.7 %copy-start.18 = (bf16[1024,768]{1,0:T(8,128)(2,1)S(1)}, bf16[1024,768]{1,0:T(8,128)(2,1)}, u32[]{:S(2)}) copy-start(bf16[1024,768]{1,0:T(8,128)(2,1)} %param.39) | copy-start | bytes 4718596
  7.2 69.6 %all-gather.8.cloned.1.call-start = ((), (), s32[]{:S(2)}) async-start(), calls=%async_computation.4 | async-start | bytes 4055040 | tf_op jit(solution)/shard_map/all_gather | solution.py:123
  13.2 141.2 %all-gather.10.cloned.1.call-start = ((), (), s32[]{:S(2)}) async-start(), calls=%async_computation.5 | async-start | bytes 1216512 | tf_op jit(solution)/shard_map/all_gather | solution.py:123
  14.6 184.6 %all-gather.12.cloned.1.call-start = ((), (), s32[]{:S(2)}) async-start(), calls=%async_computation.6 | async-start | bytes 4866048 | tf_op jit(solution)/shard_map/all_gather | solution.py:123
  15.4 249.1 %all-gather.14.cloned.1.call-start = ((), (), s32[]{:S(2)}) async-start(), calls=%async_computation.7 | async-start | bytes 4866048 | tf_op jit(solution)/shard_map/all_gather | solution.py:123
  17.1 482.5 %all-gather.16.cloned.1.call-start = ((), (), s32[]{:S(2)}) async-start(), calls=%async_computation.10 | async-start | bytes 1622016 | tf_op jit(solution)/shard_map/all_gather | solution.py:230
  43.0 50.1 %copy-start.14 = (bf16[1024,768]{1,0:T(8,128)(2,1)}, bf16[1024,768]{1,0:T(8,128)(2,1)S(1)}, u32[]{:S(2)}) copy-start(bf16[1024,768]{1,0:T(8,128)(2,1)S(1)} %constant_dynamic-slice_fusion.9) | copy-start | bytes 4718596
  93.1 3.9 copy-start.17
  149.7 4.6 copy-start.36
  158.2 1.7 copy-start.9
  158.3 146.5 %copy-start.24 = (f32[1024]{0:T(1024)}, f32[1024]{0:T(1024)S(1)}, u32[]{:S(2)}) copy-start(f32[1024]{0:T(1024)S(1)} %broadcast_multiply_fusion.5) | copy-start | bytes 12292
  160.3 144.4 %copy-start.29 = (f32[1024]{0:T(1024)}, f32[1024]{0:T(1024)S(1)}, u32[]{:S(2)}) copy-start(f32[1024]{0:T(1024)S(1)} %add_rsqrt_fusion.1) | copy-start | bytes 12292
  199.2 6.7 copy-start.27
  199.2 6.7 copy-start.32
  199.2 6.7 copy-start.33
  205.9 58.5 %copy-start.35 = (f32[768]{0:T(1024)S(1)}, f32[768]{0:T(1024)}, u32[]{:S(2)}) copy-start(f32[768]{0:T(1024)} %convert_element_type.111) | copy-start | bytes 9220
  273.9 1.4 copy-start.8
  273.9 1.4 copy-start.26
  274.3 2.4 copy-start.31
  275.3 4.0 copy-start.41
  276.7 17.4 %slice-start = ((s8[4718592]{0:T(1024)(128)(4,1)}), s8[4194304]{0:T(1024)(128)(4,1)S(1)}, s32[]{:S(2)}) async-start(s8[4718592]{0:T(1024)(128)(4,1)} %bitcast.214), calls=%async_computation.13 | async-start | bytes 8388608
  279.4 14.7 %copy-start.19 = (bf16[1024,768]{0,1:T(8,128)(2,1)}, bf16[1024,768]{0,1:T(8,128)(2,1)S(1)}, u32[]{:S(2)}) copy-start(bf16[1024,768]{0,1:T(8,128)(2,1)S(1)} %get-tuple-element.291) | copy-start | bytes 4718596
  279.4 14.7 %copy-start.10 = (f32[1024,768]{0,1:T(8,128)S(1)}, f32[1024,768]{0,1:T(8,128)}, u32[]{:S(2)}) copy-start(f32[1024,768]{0,1:T(8,128)} %copy-done.9) | copy-start | bytes 9437188
  279.4 14.7 %slice-start.1 = ((s8[4718592]{0:T(1024)(128)(4,1)}), s8[524288]{0:T(1024)(128)(4,1)S(1)}, s32[]{:S(2)}) async-start(s8[4718592]{0:T(1024)(128)(4,1)} %bitcast.214), calls=%async_computation.14 | async-start | bytes 1048576
  329.7 3.1 copy-start.4
  332.8 4.0 copy-start.3
  343.6 7.1 copy-start.11
  350.7 2.0 copy-start.2
  350.7 2.0 copy-start.5
  352.8 1.2 copy-start.12
  354.0 1.1 copy-start.6
  355.4 3.1 copy-start.4
  358.5 4.0 copy-start.3
  369.4 7.1 copy-start.11
  376.5 2.0 copy-start.2
  376.5 2.0 copy-start.5
  378.5 1.2 copy-start.12
  379.8 1.1 copy-start.6
  380.9 3.6 copy-start.22
  380.9 3.6 copy-start.23
  385.2 159.9 %reduce-scatter.15.cloned.1.call-start = ((), (), s32[]{:S(2)}) async-start(), calls=%async_computation.12 | async-start | bytes 3244032
  391.4 3.7 copy-start.7
  391.4 281.5 %reduce-scatter.13.cloned.1.call-start = ((), (), s32[]{:S(2)}) async-start(), calls=%async_computation.11 | async-start | bytes 8110080
  391.9 4.8 copy-start.13
  399.7 1.4 copy-start.15
  401.1 3.9 copy-start.21
  416.6 0.7 copy-start.25
  416.6 0.7 copy-start.28
  416.6 0.7 copy-start.30
  416.6 0.7 copy-start.34
  416.7 397.9 %reduce-scatter.9.cloned.1.call-start = ((), (), s32[]{:S(2)}) async-start(), calls=%async_computation.8 | async-start | bytes 9732096 | tf_op jit(solution)/shard_map/reduce_scatter | solution.py:205
  449.5 1.4 copy-start.20
  449.5 506.7 %reduce-scatter.11.cloned.1.call-start = ((), (), s32[]{:S(2)}) async-start(), calls=%async_computation.9 | async-start | bytes 9732096 | tf_op jit(solution)/shard_map/reduce_scatter | solution.py:205
  483.0 1.4 copy-start.16
  486.0 470.2 %copy-start.1 = (bf16[768,768]{1,0:T(8,128)(2,1)S(1)}, bf16[768,768]{1,0:T(8,128)(2,1)}, u32[]{:S(2)}) copy-start(bf16[768,768]{1,0:T(8,128)(2,1)} %param.33) | copy-start | bytes 3538948
Sparse Core Ops, SparseCore 0:
  13.3 63.5 all-gather.7
  80.4 52.7 all-gather.9
  136.6 62.4 all-gather.11
  202.5 61.9 all-gather.13
  385.4 53.2 all-gather.15
  444.0 101.0 reduce-scatter.14
  550.8 122.1 reduce-scatter.12
  679.4 135.0 reduce-scatter.8
  821.0 135.1 reduce-scatter.10
